TPU v7x, 32 devices: a whole 2x2x4 slice. The times are simulated.
32 devices in a mesh: wide: 8 (over z, x), narrow: 4 (over y, core).
Axes of the slice: x: 2, y: 2, z: 4, core: 2. Of those that a mesh axis runs over, the one named last changes fastest.
Arguments:
- pressure: float32 [1024, 128], P(('wide', 'narrow')), may hold values from -6 to 6
- right_side: float32 [1024, 128], P(('wide', 'narrow')), may hold values from -6 to 6
- concentration: float32 [1024, 128], P(('wide', 'narrow')), may hold values from 0 to 1
- pore_volume: float32 [1024, 128], P(('wide', 'narrow')), may hold values from 0.5 to 2
- well_rate: float32 [1024, 128], P(('wide', 'narrow')), may hold values from 0.02 to 0.5
- inject_conc: float32 [1024, 128], P(('wide', 'narrow')), may hold values from 0 to 1
- transmissibility: float32 [6, 131072], P(None, ('wide', 'narrow')), may hold values from 0.1 to 1
- face_neighbor: int32 [6, 1024], P(None, ('wide', 'narrow')), may hold values from 0 to 56, as said below
- sub_matrix: bfloat16 [2048, 4, 128, 128], P(('wide', 'narrow')), as said below
- sub_columns: int32 [2048, 4], P(('wide', 'narrow')), may hold values from 0 to 63, as said below
- send_blocks: int32 [32, 4, 8], P(('wide', 'narrow')), may hold values from 0 to 31, as said below
- send_counts: int32 [32, 4], P(('wide', 'narrow')), may hold values from 1 to 8, as said below
- basis_weights: bfloat16 [8192, 4096], P(('wide', 'narrow')), may hold values from -0.09375 to 0.09375
- coarse_index: int32 [8192], P(('wide', 'narrow')), may hold values from 0 to 4095, as said below
- coarse_inverse: float32 [4096, 512], P(('wide', 'narrow')), may hold values from -0.25 to 0.25
Outputs:
- pressure_new: float32 [1024, 128], P(('wide', 'narrow'))
- concentration_new: float32 [1024, 128], P(('wide', 'narrow'))
Inputs may be any that keep to these rules, and one draw needn't show every extreme that they name: `send_blocks`: local block indices below 32. `send_counts`: between 1 and 8; the first subdomain sends 8 blocks to every neighbour and the last sends one. `sub_columns`: slot 0 of each row block names the row block itself. `face_neighbor`: each owned block's faces name owned blocks or the first received block from some neighbour. `coarse_index`: a subdomain's functions may be owned by any index of wide, and may repeat. `sub_matrix`: the diagonal of each row block's first stored block lies between 0.9 and 2.1.
All inputs are finite; a program needn't handle non-finite values.
Results may differ from a plain program's by a relative error of at most 0.00225.
The roundings to bfloat16 on the way count: a program that leaves them out, or rounds other values in their place, can miss the bound.
Values may be sent and summed in bfloat16 or wider, within the bound.
A program may use at most 64 MiB of HBM per device.

v0:
```python
import jax
import jax.numpy as jnp
from jax import lax
from jax.sharding import PartitionSpec as P

SWEEPS = 4


shift_offsets = (2, 1, -1, -2)
courant = 0.9


def from_behind(value, axis, steps):
    count = lax.axis_size(axis)
    leading, last = (max(0, -steps), min(count, count - steps))
    return lax.ppermute(value, axis, [(source, source + steps) for source in range(leading, last)])


def block_product(matrix, columns, vector_b):
    picked = vector_b[columns]
    return jnp.einsum("rkij,rkj->ri", matrix, picked, preferred_element_type=jnp.float32)


def outgoing_one(owned_rows, send_blocks, send_counts):
    slot_count = send_blocks.shape[-1]
    active = jnp.arange(slot_count)[None, :] < send_counts[0][:, None]
    picked = owned_rows[send_blocks[0]]
    return jnp.where(active[:, :, None], picked, jnp.zeros_like(picked))


def with_rims(owned_list, send_blocks, send_counts, mover):
    packed = [outgoing_one(owned_rows, send_blocks, send_counts) for owned_rows in owned_list]
    arrived = [[owned_rows] for owned_rows in owned_list]
    for position, offset in enumerate(shift_offsets):
        moved_rows = mover([sent_rows[position] for sent_rows in packed], offset)
        for target, portion in zip(arrived, moved_rows):
            target.append(portion)
    return [jnp.concatenate(target, axis=0) for target in arrived]


def local(
    pressure,
    right_side,
    concentration,
    pore_volume,
    well_rate,
    inject_conc,
    transmissibility,
    face_neighbor,
    sub_matrix,
    sub_columns,
    send_blocks,
    send_counts,
    basis_weights,
    coarse_index,
    coarse_inverse,
):
    owned_count = pressure.shape[0]
    pressure_b = pressure.astype(jnp.bfloat16)
    ext_pressure = with_rims(
        [pressure_b],
        send_blocks,
        send_counts,
        lambda members, offset: (from_behind(members[0], "wide", offset),),
    )[0]
    residual = right_side - block_product(
        sub_matrix[:owned_count], sub_columns[:owned_count], ext_pressure
    )
    residual_b = residual.astype(jnp.bfloat16)
    local_coarse = jnp.dot(
        basis_weights, residual_b.reshape(-1), preferred_element_type=jnp.float32
    )
    coarse_width = coarse_inverse.shape[1]
    wide_count = lax.axis_size("wide")
    coarse_total = coarse_width * wide_count
    ext_residual = with_rims(
        [residual_b],
        send_blocks,
        send_counts,
        lambda members, offset: (from_behind(members[0], "wide", offset),),
    )[0]
    diagonal = jnp.diagonal(sub_matrix[:, 0], axis1=1, axis2=2).astype(jnp.float32)
    target_rows = ext_residual.astype(jnp.float32)
    update = jnp.zeros(target_rows.shape, jnp.float32)
    for turn_index in range(SWEEPS):
        update = (
            update
            + (target_rows - block_product(sub_matrix, sub_columns, update.astype(jnp.bfloat16)))
            / diagonal
        )
    partial_value = jnp.zeros((coarse_total,), jnp.float32).at[coarse_index].add(local_coarse)
    summed = lax.psum(partial_value, ("wide", "narrow"))
    owner_block = lax.dynamic_slice_in_dim(
        summed, lax.axis_index("wide") * coarse_width, coarse_width
    )
    block_inverse = lax.all_gather(coarse_inverse, "narrow", axis=0, tiled=True)
    owner_values = jnp.dot(block_inverse, owner_block, precision=lax.Precision.HIGHEST)
    coarse_values = lax.all_gather(owner_values, "wide", axis=0, tiled=True)
    picked_coarse = coarse_values.astype(jnp.bfloat16)[coarse_index]
    correction = jnp.dot(picked_coarse, basis_weights, preferred_element_type=jnp.float32)
    pressure_next = pressure + update[:owned_count] + correction.reshape(owned_count, -1)
    ext_next, ext_conc = with_rims(
        [pressure_next, concentration],
        send_blocks,
        send_counts,
        lambda members, offset: from_behind((members[0], members[1]), "wide", offset),
    )
    face_count = face_neighbor.shape[0]
    near_pressure = ext_next[face_neighbor].reshape(face_count, -1)
    near_conc = ext_conc[face_neighbor].reshape(face_count, -1)
    own_pressure = pressure_next.reshape(1, -1)
    conc_flat = concentration.reshape(-1)
    face_flux = transmissibility * (own_pressure - near_pressure)
    outward = jnp.maximum(face_flux, 0.0)
    inward = jnp.minimum(face_flux, 0.0)
    advection = jnp.sum(outward * conc_flat[None, :] + inward * near_conc, axis=0)
    outflow = jnp.sum(outward, axis=0)
    volume_flat = pore_volume.reshape(-1)
    rate_flat = well_rate.reshape(-1)
    cell_rate = (outflow + rate_flat) / volume_flat
    rate_top = lax.pmax(jnp.max(cell_rate), ("wide", "narrow"))
    time_step = courant / rate_top
    conc_next = conc_flat + time_step / volume_flat * (
        rate_flat * (inject_conc.reshape(-1) - conc_flat) - advection
    )
    return (pressure_next, conc_next.reshape(owned_count, -1))


def solution(mesh):
    return jax.shard_map(
        local,
        mesh=mesh,
        in_specs=(
            P(("wide", "narrow"), None),
            P(("wide", "narrow"), None),
            P(("wide", "narrow"), None),
            P(("wide", "narrow"), None),
            P(("wide", "narrow"), None),
            P(("wide", "narrow"), None),
            P(None, ("wide", "narrow")),
            P(None, ("wide", "narrow")),
            P(("wide", "narrow"), None, None, None),
            P(("wide", "narrow"), None),
            P(("wide", "narrow"), None, None),
            P(("wide", "narrow"), None),
            P(("wide", "narrow"), None),
            P(("wide", "narrow")),
            P(("wide", "narrow"), None),
        ),
        out_specs=(P(("wide", "narrow"), None), P(("wide", "narrow"), None)),
        check_vma=False,
    )
```

profile of v0, /device:TPU:0, one launch (start us, length us, event | category | flops | bytes accessed | tf_op | source)
XLA Modules:
  0.0 232.3 jit_solution(17184199817668447989)
XLA Ops:
  10.3 4.9 %collective-permute-start = (bf16[8,128]{1,0:T(8,128)(2,1)S(1)}, bf16[8,128]{1,0:T(8,128)(2,1)S(1)}, u32[]{:S(2)}, u32[]{:S(2)}) collective-permute-start(bf16[8,128]{1,0:T(8,128)(2,1)S(1)} %get-tuple-element.29), channel_id=1, source_target_pairs={{0,8},{4,12},{8,16},{12,20},{16,24},{20,28},{1,9},{5,13},{9,17},{1... | collective-permute-start | bytes 6152 | tf_op jit(solution)/shard_map/ppermute | solution.py:16
  15.2 3.4 %collective-permute-start.1 = (bf16[8,128]{1,0:T(8,128)(2,1)S(1)}, bf16[8,128]{1,0:T(8,128)(2,1)S(1)}, u32[]{:S(2)}, u32[]{:S(2)}) collective-permute-start(bf16[8,128]{1,0:T(8,128)(2,1)S(1)} %get-tuple-element.28), channel_id=1, source_target_pairs={{0,4},{4,8},{8,12},{12,16},{16,20},{20,24},{24,28},{1,5},{5,9},{9,... | collective-permute-start | bytes 6152 | tf_op jit(solution)/shard_map/ppermute | solution.py:16
  18.6 1.3 collective-permute-start.2
  19.9 1.3 collective-permute-start.3
  23.5 3.2 %slice.70 = bf16[64,1,128,128]{3,2,1,0:T(8,128)(2,1)} slice(bf16[64,4,128,128]{3,2,1,0:T(8,128)(2,1)} %param.23), slice={[0:64], [0:1], [0:128], [0:128]} | slice | bytes 4194304 | tf_op jit(solution)/shard_map/slice | solution.py:82
  26.7 5.3 %copy.38 = bf16[64,1,128,128]{0,3,2,1:T(8,128)(2,1)} copy(bf16[64,1,128,128]{3,2,1,0:T(8,128)(2,1)} %slice.70) | data formatting | bytes 4194304
  32.1 1.9 gather_fusion.4
  35.2 5.7 %fusion.8 = f32[64,1,128,1]{2,1,3,0:T(1,128)S(1)} fusion(bf16[64,4,128,128]{3,2,1,0:T(8,128)(2,1)} %param.23, bf16[64,4,128,1]{2,1,0,3:T(4,128)(2,1)S(1)} %bitcast.134), kind=kOutput, calls=%fused_computation.23 | convolution fusion | flops 8388608 | bytes 8486912 | tf_op jit(solution)/shard_map/rkij,rkj->ri/dot_general | solution.py:21
  42.4 3.4 %fusion = f32[32,1,128,1]{2,1,3,0:T(1,128)S(1)} fusion(bf16[64,4,128,128]{3,2,1,0:T(8,128)(2,1)} %param.23, bf16[32,4,128,1]{2,1,0,3:T(4,128)(2,1)S(1)} %bitcast.143), kind=kOutput, calls=%fused_computation.14 | convolution fusion | flops 4194304 | bytes 4243456 | tf_op jit(solution)/shard_map/rkij,rkj->ri/dot_general | solution.py:21
  46.5 6.3 %collective-permute-start.4 = (bf16[8,128]{1,0:T(8,128)(2,1)S(1)}, bf16[8,128]{1,0:T(8,128)(2,1)S(1)}, u32[]{:S(2)}, u32[]{:S(2)}) collective-permute-start(bf16[8,128]{1,0:T(8,128)(2,1)S(1)} %get-tuple-element.25), channel_id=1, source_target_pairs={{0,8},{4,12},{8,16},{12,20},{16,24},{20,28},{1,9},{5,13},{9,17},{1... | collective-permute-start | bytes 6152 | tf_op jit(solution)/shard_map/ppermute | solution.py:16
  53.5 2.0 scatter_custom_fusion
  55.4 40.0 %psum.7 = f32[4096]{0:T(1024)S(1)} all-reduce(f32[4096]{0:T(1024)S(1)} %scatter_custom_fusion), channel_id=1, replica_groups=mesh['wide'=8,'narrow'=4] {'wide','narrow'}, use_global_device_ids=true, to_apply=%region_1.2 | all-reduce | flops 4096 | bytes 32768 | tf_op jit(solution)/shard_map/psum | solution.py:92
  95.4 4.2 %collective-permute-start.5 = (bf16[8,128]{1,0:T(8,128)(2,1)S(1)}, bf16[8,128]{1,0:T(8,128)(2,1)S(1)}, u32[]{:S(2)}, u32[]{:S(2)}) collective-permute-start(bf16[8,128]{1,0:T(8,128)(2,1)S(1)} %get-tuple-element.24), channel_id=1, source_target_pairs={{0,4},{4,8},{8,12},{12,16},{16,20},{20,24},{24,28},{1,5},{5,9},{9,... | collective-permute-start | bytes 6152 | tf_op jit(solution)/shard_map/ppermute | solution.py:16
  99.6 1.3 collective-permute-start.6
  100.9 1.5 collective-permute-start.7
  102.5 2.6 %collective-permute-done.6 = bf16[8,128]{1,0:T(8,128)(2,1)S(1)} collective-permute-done((bf16[8,128]{1,0:T(8,128)(2,1)S(1)}, bf16[8,128]{1,0:T(8,128)(2,1)S(1)}, u32[]{:S(2)}, u32[]{:S(2)}) %collective-permute-start.6) | collective-permute-done | bytes 2080 | tf_op jit(solution)/shard_map/ppermute | solution.py:16
  105.1 1.4 collective-permute-done.7
  107.4 5.6 %fusion.6 = f32[64,1,128,1]{2,1,3,0:T(1,128)S(1)} fusion(bf16[64,4,128,128]{3,2,1,0:T(8,128)(2,1)} %param.23, bf16[64,4,128,1]{2,1,0,3:T(4,128)(2,1)S(1)} %bitcast.135), kind=kOutput, calls=%fused_computation.21 | convolution fusion | flops 8388608 | bytes 8486912 | tf_op jit(solution)/shard_map/rkij,rkj->ri/dot_general | solution.py:21
  113.9 5.6 %fusion.4 = f32[64,1,128,1]{2,1,3,0:T(1,128)S(1)} fusion(bf16[64,4,128,128]{3,2,1,0:T(8,128)(2,1)} %param.23, bf16[64,4,128,1]{2,1,0,3:T(4,128)(2,1)S(1)} %bitcast.136), kind=kOutput, calls=%fused_computation.19 | convolution fusion | flops 8388608 | bytes 8486912 | tf_op jit(solution)/shard_map/rkij,rkj->ri/dot_general | solution.py:21
  120.5 5.6 %fusion.2 = f32[64,1,128,1]{2,1,3,0:T(1,128)S(1)} fusion(bf16[64,4,128,128]{3,2,1,0:T(8,128)(2,1)} %param.23, bf16[64,4,128,1]{2,1,0,3:T(4,128)(2,1)S(1)} %bitcast.133), kind=kOutput, calls=%fused_computation.17 | convolution fusion | flops 8388608 | bytes 8486912 | tf_op jit(solution)/shard_map/rkij,rkj->ri/dot_general | solution.py:21
  126.1 2.2 convolution_bitcast_fusion
  128.3 26.0 %all-gather = bf16[8,1,512]{2,1,0:T(2,128)(2,1)S(1)} all-gather(bf16[1,1,512]{2,1,0:T(2,128)(2,1)S(1)} %convolution_bitcast_fusion), channel_id=1, replica_groups=mesh['wide'=8,'narrow'=4] {'wide'}, dimensions={0}, use_global_device_ids=true | all-gather | bytes 9216 | tf_op jit(solution)/shard_map/all_gather | solution.py:98
  154.4 1.9 gather_fusion.8
  157.4 2.1 collective-permute-start.8
  159.6 1.8 collective-permute-start.9
  163.9 6.5 %collective-permute-start.12 = (f32[8,128]{1,0:T(8,128)S(1)}, f32[8,128]{1,0:T(8,128)S(1)}, u32[]{:S(2)}, u32[]{:S(2)}) collective-permute-start(f32[8,128]{1,0:T(8,128)S(1)} %get-tuple-element.17), channel_id=1, source_target_pairs={{0,8},{4,12},{8,16},{12,20},{16,24},{20,28},{1,9},{5,13},{9,17},{1... | collective-permute-start | bytes 12296 | tf_op jit(solution)/shard_map/ppermute | solution.py:16
  170.4 2.6 %collective-permute-start.13 = (f32[8,128]{1,0:T(8,128)S(1)}, f32[8,128]{1,0:T(8,128)S(1)}, u32[]{:S(2)}, u32[]{:S(2)}) collective-permute-start(f32[8,128]{1,0:T(8,128)S(1)} %get-tuple-element.16), channel_id=1, source_target_pairs={{0,4},{4,8},{8,12},{12,16},{16,20},{20,24},{24,28},{1,5},{5,9},{9,... | collective-permute-start | bytes 12296 | tf_op jit(solution)/shard_map/ppermute | solution.py:16
  173.1 1.3 collective-permute-start.14
  174.4 1.3 collective-permute-start.15
  175.8 3.5 %collective-permute-done.14 = f32[8,128]{1,0:T(8,128)S(1)} collective-permute-done((f32[8,128]{1,0:T(8,128)S(1)}, f32[8,128]{1,0:T(8,128)S(1)}, u32[]{:S(2)}, u32[]{:S(2)}) %collective-permute-start.14) | collective-permute-done | bytes 4128 | tf_op jit(solution)/shard_map/ppermute | solution.py:16
  180.0 2.7 %collective-permute-done.15 = f32[8,128]{1,0:T(8,128)S(1)} collective-permute-done((f32[8,128]{1,0:T(8,128)S(1)}, f32[8,128]{1,0:T(8,128)S(1)}, u32[]{:S(2)}, u32[]{:S(2)}) %collective-permute-start.15) | collective-permute-done | bytes 4128 | tf_op jit(solution)/shard_map/ppermute | solution.py:16
  184.2 39.9 %pmax.7 = f32[]{:T(128)} all-reduce(f32[]{:T(128)} %fusion.16), channel_id=1, replica_groups=mesh['wide'=8,'narrow'=4] {'wide','narrow'}, use_global_device_ids=true, to_apply=%region_4.5 | all-reduce | flops 1 | bytes 8 | tf_op jit(solution)/shard_map/pmax | solution.py:121
  (112 shorter events, 18.6 us)
Async XLA Ops:
  7.2 45.6 %copy-start = (bf16[256,4096]{1,0:T(8,128)(2,1)S(1)}, bf16[256,4096]{1,0:T(8,128)(2,1)}, u32[]{:S(2)}) copy-start(bf16[256,4096]{1,0:T(8,128)(2,1)} %param.27) | copy-start | bytes 6291460
  7.2 118.9 %all-gather.3.cloned.1.call-start = ((), (), s32[]{:S(2)}) async-start(), calls=%async_computation | async-start | bytes 1310720 | tf_op jit(solution)/shard_map/all_gather | solution.py:96
  10.3 31.3 %collective-permute-start = (bf16[8,128]{1,0:T(8,128)(2,1)S(1)}, bf16[8,128]{1,0:T(8,128)(2,1)S(1)}, u32[]{:S(2)}, u32[]{:S(2)}) collective-permute-start(bf16[8,128]{1,0:T(8,128)(2,1)S(1)} %get-tuple-element.29), channel_id=1, source_target_pairs={{0,8},{4,12},{8,16},{12,20},{16,24},{20,28},{1,9},{5,13},{9,17},{1... | collective-permute-start | bytes 6152 | tf_op jit(solution)/shard_map/ppermute | solution.py:16
  15.2 26.4 %collective-permute-start.1 = (bf16[8,128]{1,0:T(8,128)(2,1)S(1)}, bf16[8,128]{1,0:T(8,128)(2,1)S(1)}, u32[]{:S(2)}, u32[]{:S(2)}) collective-permute-start(bf16[8,128]{1,0:T(8,128)(2,1)S(1)} %get-tuple-element.28), channel_id=1, source_target_pairs={{0,4},{4,8},{8,12},{12,16},{16,20},{20,24},{24,28},{1,5},{5,9},{9,... | collective-permute-start | bytes 6152 | tf_op jit(solution)/shard_map/ppermute | solution.py:16
  18.6 23.0 %collective-permute-start.2 = (bf16[8,128]{1,0:T(8,128)(2,1)S(1)}, bf16[8,128]{1,0:T(8,128)(2,1)S(1)}, u32[]{:S(2)}, u32[]{:S(2)}) collective-permute-start(bf16[8,128]{1,0:T(8,128)(2,1)S(1)} %get-tuple-element.27), channel_id=1, source_target_pairs={{4,0},{8,4},{12,8},{16,12},{20,16},{24,20},{28,24},{5,1},{9,5},{13... | collective-permute-start | bytes 6152 | tf_op jit(solution)/shard_map/ppermute | solution.py:16
  19.9 21.8 %collective-permute-start.3 = (bf16[8,128]{1,0:T(8,128)(2,1)S(1)}, bf16[8,128]{1,0:T(8,128)(2,1)S(1)}, u32[]{:S(2)}, u32[]{:S(2)}) collective-permute-start(bf16[8,128]{1,0:T(8,128)(2,1)S(1)} %get-tuple-element.26), channel_id=1, source_target_pairs={{8,0},{12,4},{16,8},{20,12},{24,16},{28,20},{9,1},{13,5},{17,9},{2... | collective-permute-start | bytes 6152 | tf_op jit(solution)/shard_map/ppermute | solution.py:16
  26.7 14.2 %copy-start.9 = (s32[6,32]{1,0:T(8,128)S(1)}, s32[6,32]{1,0:T(8,128)}, u32[]{:S(2)}) copy-start(s32[6,32]{1,0:T(8,128)} %param.22) | copy-start | bytes 2308
  26.7 14.3 %copy-start.1 = (f32[32,128]{1,0:T(8,128)S(1)}, f32[32,128]{1,0:T(8,128)}, u32[]{:S(2)}) copy-start(f32[32,128]{1,0:T(8,128)} %param.17) | copy-start | bytes 49156
  32.1 13.7 %copy-start.7 = (f32[32,128]{1,0:T(8,128)S(1)}, f32[32,128]{1,0:T(8,128)}, u32[]{:S(2)}) copy-start(f32[32,128]{1,0:T(8,128)} %param.16) | copy-start | bytes 49156
  46.5 56.0 %collective-permute-start.4 = (bf16[8,128]{1,0:T(8,128)(2,1)S(1)}, bf16[8,128]{1,0:T(8,128)(2,1)S(1)}, u32[]{:S(2)}, u32[]{:S(2)}) collective-permute-start(bf16[8,128]{1,0:T(8,128)(2,1)S(1)} %get-tuple-element.25), channel_id=1, source_target_pairs={{0,8},{4,12},{8,16},{12,20},{16,24},{20,28},{1,9},{5,13},{9,17},{1... | collective-permute-start | bytes 6152 | tf_op jit(solution)/shard_map/ppermute | solution.py:16
  95.4 7.1 %collective-permute-start.5 = (bf16[8,128]{1,0:T(8,128)(2,1)S(1)}, bf16[8,128]{1,0:T(8,128)(2,1)S(1)}, u32[]{:S(2)}, u32[]{:S(2)}) collective-permute-start(bf16[8,128]{1,0:T(8,128)(2,1)S(1)} %get-tuple-element.24), channel_id=1, source_target_pairs={{0,4},{4,8},{8,12},{12,16},{16,20},{20,24},{24,28},{1,5},{5,9},{9,... | collective-permute-start | bytes 6152 | tf_op jit(solution)/shard_map/ppermute | solution.py:16
  99.6 5.5 %collective-permute-start.6 = (bf16[8,128]{1,0:T(8,128)(2,1)S(1)}, bf16[8,128]{1,0:T(8,128)(2,1)S(1)}, u32[]{:S(2)}, u32[]{:S(2)}) collective-permute-start(bf16[8,128]{1,0:T(8,128)(2,1)S(1)} %get-tuple-element.23), channel_id=1, source_target_pairs={{4,0},{8,4},{12,8},{16,12},{20,16},{24,20},{28,24},{5,1},{9,5},{13... | collective-permute-start | bytes 6152 | tf_op jit(solution)/shard_map/ppermute | solution.py:16
  100.9 5.6 %collective-permute-start.7 = (bf16[8,128]{1,0:T(8,128)(2,1)S(1)}, bf16[8,128]{1,0:T(8,128)(2,1)S(1)}, u32[]{:S(2)}, u32[]{:S(2)}) collective-permute-start(bf16[8,128]{1,0:T(8,128)(2,1)S(1)} %get-tuple-element.22), channel_id=1, source_target_pairs={{8,0},{12,4},{16,8},{20,12},{24,16},{28,20},{9,1},{13,5},{17,9},{2... | collective-permute-start | bytes 6152 | tf_op jit(solution)/shard_map/ppermute | solution.py:16
  119.5 37.2 %copy-start.6 = (f32[32,128]{1,0:T(8,128)S(1)}, f32[32,128]{1,0:T(8,128)}, u32[]{:S(2)}) copy-start(f32[32,128]{1,0:T(8,128)} %param.15) | copy-start | bytes 49156
  119.5 63.9 %copy-start.3 = (f32[6,4096]{1,0:T(8,128)S(1)}, f32[6,4096]{1,0:T(8,128)}, u32[]{:S(2)}) copy-start(f32[6,4096]{1,0:T(8,128)} %param.21) | copy-start | bytes 294916
  119.5 64.0 %copy-start.4 = (f32[32,128]{1,0:T(8,128)S(1)}, f32[32,128]{1,0:T(8,128)}, u32[]{:S(2)}) copy-start(f32[32,128]{1,0:T(8,128)} %param.19) | copy-start | bytes 49156
  119.6 64.0 %copy-start.5 = (f32[32,128]{1,0:T(8,128)S(1)}, f32[32,128]{1,0:T(8,128)}, u32[]{:S(2)}) copy-start(f32[32,128]{1,0:T(8,128)} %param.18) | copy-start | bytes 49156
  119.6 105.2 %copy-start.8 = (f32[32,128]{1,0:T(8,128)S(1)}, f32[32,128]{1,0:T(8,128)}, u32[]{:S(2)}) copy-start(f32[32,128]{1,0:T(8,128)} %param.20) | copy-start | bytes 49156
  156.7 68.7 %copy-start.2 = (f32[32,128]{1,0:T(8,128)}, f32[32,128]{1,0:T(8,128)S(1)}, u32[]{:S(2)}) copy-start(f32[32,128]{1,0:T(8,128)S(1)} %get-tuple-element.5) | copy-start | bytes 49156
  157.4 13.0 %collective-permute-start.8 = (f32[8,128]{1,0:T(8,128)S(1)}, f32[8,128]{1,0:T(8,128)S(1)}, u32[]{:S(2)}, u32[]{:S(2)}) collective-permute-start(f32[8,128]{1,0:T(8,128)S(1)} %get-tuple-element.21), channel_id=1, source_target_pairs={{0,8},{4,12},{8,16},{12,20},{16,24},{20,28},{1,9},{5,13},{9,17},{1... | collective-permute-start | bytes 12296 | tf_op jit(solution)/shard_map/ppermute | solution.py:16
  159.6 13.5 %collective-permute-start.9 = (f32[8,128]{1,0:T(8,128)S(1)}, f32[8,128]{1,0:T(8,128)S(1)}, u32[]{:S(2)}, u32[]{:S(2)}) collective-permute-start(f32[8,128]{1,0:T(8,128)S(1)} %get-tuple-element.20), channel_id=1, source_target_pairs={{0,4},{4,8},{8,12},{12,16},{16,20},{20,24},{24,28},{1,5},{5,9},{9,... | collective-permute-start | bytes 12296 | tf_op jit(solution)/shard_map/ppermute | solution.py:16
  161.3 13.1 %collective-permute-start.10 = (f32[8,128]{1,0:T(8,128)S(1)}, f32[8,128]{1,0:T(8,128)S(1)}, u32[]{:S(2)}, u32[]{:S(2)}) collective-permute-start(f32[8,128]{1,0:T(8,128)S(1)} %get-tuple-element.19), channel_id=1, source_target_pairs={{4,0},{8,4},{12,8},{16,12},{20,16},{24,20},{28,24},{5,1},{9,5},{13... | collective-permute-start | bytes 12296 | tf_op jit(solution)/shard_map/ppermute | solution.py:16
  162.6 13.1 %collective-permute-start.11 = (f32[8,128]{1,0:T(8,128)S(1)}, f32[8,128]{1,0:T(8,128)S(1)}, u32[]{:S(2)}, u32[]{:S(2)}) collective-permute-start(f32[8,128]{1,0:T(8,128)S(1)} %get-tuple-element.18), channel_id=1, source_target_pairs={{8,0},{12,4},{16,8},{20,12},{24,16},{28,20},{9,1},{13,5},{17,9},{2... | collective-permute-start | bytes 12296 | tf_op jit(solution)/shard_map/ppermute | solution.py:16
  163.9 11.8 %collective-permute-start.12 = (f32[8,128]{1,0:T(8,128)S(1)}, f32[8,128]{1,0:T(8,128)S(1)}, u32[]{:S(2)}, u32[]{:S(2)}) collective-permute-start(f32[8,128]{1,0:T(8,128)S(1)} %get-tuple-element.17), channel_id=1, source_target_pairs={{0,8},{4,12},{8,16},{12,20},{16,24},{20,28},{1,9},{5,13},{9,17},{1... | collective-permute-start | bytes 12296 | tf_op jit(solution)/shard_map/ppermute | solution.py:16
  170.4 5.3 %collective-permute-start.13 = (f32[8,128]{1,0:T(8,128)S(1)}, f32[8,128]{1,0:T(8,128)S(1)}, u32[]{:S(2)}, u32[]{:S(2)}) collective-permute-start(f32[8,128]{1,0:T(8,128)S(1)} %get-tuple-element.16), channel_id=1, source_target_pairs={{0,4},{4,8},{8,12},{12,16},{16,20},{20,24},{24,28},{1,5},{5,9},{9,... | collective-permute-start | bytes 12296 | tf_op jit(solution)/shard_map/ppermute | solution.py:16
  173.1 6.2 %collective-permute-start.14 = (f32[8,128]{1,0:T(8,128)S(1)}, f32[8,128]{1,0:T(8,128)S(1)}, u32[]{:S(2)}, u32[]{:S(2)}) collective-permute-start(f32[8,128]{1,0:T(8,128)S(1)} %get-tuple-element.15), channel_id=1, source_target_pairs={{4,0},{8,4},{12,8},{16,12},{20,16},{24,20},{28,24},{5,1},{9,5},{13... | collective-permute-start | bytes 12296 | tf_op jit(solution)/shard_map/ppermute | solution.py:16
  174.4 8.3 %collective-permute-start.15 = (f32[8,128]{1,0:T(8,128)S(1)}, f32[8,128]{1,0:T(8,128)S(1)}, u32[]{:S(2)}, u32[]{:S(2)}) collective-permute-start(f32[8,128]{1,0:T(8,128)S(1)} %get-tuple-element.14), channel_id=1, source_target_pairs={{8,0},{12,4},{16,8},{20,12},{24,16},{28,20},{9,1},{13,5},{17,9},{2... | collective-permute-start | bytes 12296 | tf_op jit(solution)/shard_map/ppermute | solution.py:16
Sparse Core Ops, SparseCore 0:
  21.3 20.1 all-gather.2
where the time goes:
time: 233 us; the launch traced here: 232 us
  blocking collectives  106 us (45%)
  starting transfers between devices  42.3 us (18%)
  matrix products  29.2 us (13%)
  local copies, waits for them, and re-layouts  21.3 us (9%)
  between operations  15.3 us (7%)
  waiting for transfers between devices  10.2 us (4%)
  other arithmetic  8.02 us (3%)
    ppermute x16, starting transfers between devices, from_behind(): lax.ppermute(value, axis, [(source, source + steps) for source in range(l...  42.3 us
    psum x1, blocking collectives, local(): summed = lax.psum(partial_value, ('wide', 'narrow'))  40 us
    pmax x1, blocking collectives, local(): rate_top = lax.pmax(jnp.max(cell_rate), ('wide', 'narrow'))  39.9 us
    all_gather x1, blocking collectives, local(): coarse_values = lax.all_gather(owner_values, 'wide', axis=0, tiled=True)  26 us
    dot_general x5, matrix products, block_product(): jnp.einsum('rkij,rkj->ri', matrix, picked, preferred_element_type=jnp.flo...  26 us
    ppermute x16, waiting for transfers between devices, from_behind(): lax.ppermute(value, axis, [(source, source + steps) for source in range(l...  10.2 us
    unnamed x35, local copies, waits for them, and re-layouts  5.47 us
  transfers between devices with their start and end apart: 17, of which 4 were waited for; matrix products, arithmetic and copies ran while one was open for 21% of the time, Pallas kernels for 0%

commit v1 on v0

v1 whole, which is shorter than its diff:
```python
import functools

import jax
import jax.numpy as jnp
from jax import lax
from jax.experimental import pallas as pl
from jax.experimental.pallas import tpu as pltpu
from jax.sharding import PartitionSpec as P

SWEEPS = 4

shift_offsets = (2, 1, -1, -2)
courant = 0.9
MESH = pl.DeviceIdType.MESH
f32, bf16 = jnp.float32, jnp.bfloat16
contract_last = (((1,), (1,)), ((), ()))
plain = (((1,), (0,)), ((), ()))


def rounded(value):
    return value.astype(bf16).astype(f32)


def kernel(
    wide_count,
    narrow_count,
    face_neighbor,
    sub_columns,
    send_blocks,
    send_counts,
    index_column,
    pressure_hbm,
    right_hbm,
    conc_hbm,
    volume_hbm,
    rate_hbm,
    inject_hbm,
    trans_hbm,
    matrix_hbm,
    basis_hbm,
    inverse_hbm,
    pressure_out,
    conc_out,
    pressure,
    right_side,
    conc,
    volume,
    rate,
    inject,
    trans,
    matrix,
    basis,
    inverse,
    load_sem,
    outbox,
    inbox,
    margin_send,
    margin_recv,
    own,
    ext_a,
    ext_b,
    target,
    diag,
    picked,
    onehot,
    partial,
    wide_in,
    wide_sum,
    narrow_in,
    value_in,
    value_mine,
    coarse_in,
    coarse_mine,
    top_mine,
    top_narrow,
    top_half,
    top_wide,
    wide_send,
    wide_recv,
    narrow_send,
    narrow_recv,
    near_p,
    near_c,
    ext_c,
    adv,
):
    w, n = lax.axis_index("wide"), lax.axis_index("narrow")
    owned, lanes = pressure.shape
    extent = ext_a.shape[0]
    slots = outbox.shape[2]
    faces = trans.shape[0]
    coarse_width = inverse.shape[1]

    loads = []
    sources = (
        (pressure_hbm, pressure),
        (conc_hbm, conc),
        (matrix_hbm.at[pl.ds(0, owned)], matrix.at[pl.ds(0, owned)]),
        (matrix_hbm.at[pl.ds(owned, extent - owned)], matrix.at[pl.ds(owned, extent - owned)]),
        (right_hbm, right_side),
        (basis_hbm, basis),
        (inverse_hbm, inverse),
        (trans_hbm, trans),
        (volume_hbm, volume),
        (rate_hbm, rate),
        (inject_hbm, inject),
    )
    for at, (source, place) in enumerate(sources):
        copy = pltpu.make_async_copy(source, place, load_sem.at[at])
        copy.start()
        loads.append(copy)

    barrier = pltpu.get_barrier_semaphore()
    for step in range(1, wide_count):
        pl.semaphore_signal(barrier, inc=1, device_id=(lax.rem(w + step, wide_count), n), device_id_type=MESH)
    for step in range(1, narrow_count):
        pl.semaphore_signal(barrier, inc=1, device_id=(w, lax.rem(n + step, narrow_count)), device_id_type=MESH)

    def margin_copy(turn, position):
        offset = shift_offsets[position]
        return pltpu.make_async_remote_copy(
            src_ref=outbox.at[turn, position],
            dst_ref=inbox.at[turn, position],
            send_sem=margin_send.at[turn, position],
            recv_sem=margin_recv.at[turn, position],
            device_id=(w + offset, n),
            device_id_type=MESH,
        )

    def reaches(offset):
        return jnp.logical_and(w + offset >= 0, w + offset < wide_count)

    slot_id = lax.broadcasted_iota(jnp.int32, (slots, lanes), 0)

    def pack(turn, rows):
        for position in range(4):
            for t in range(slots):
                outbox[turn, position, pl.ds(t, 1), :] = rows[pl.ds(send_blocks[0, position, t], 1), :]
            filled = outbox[turn, position]
            outbox[turn, position] = jnp.where(slot_id < send_counts[0, position], filled, 0.0)

    def send_margin(turn):
        for position, offset in enumerate(shift_offsets):
            @pl.when(reaches(offset))
            def _():
                margin_copy(turn, position).start()

    def take_margin(turn, place):
        for position, offset in enumerate(shift_offsets):
            rows = pl.ds(owned + position * slots, slots)

            @pl.when(reaches(-offset))
            def _():
                margin_copy(turn, position).wait_recv()
                place[rows, :] = inbox[turn, position]

            @pl.when(jnp.logical_not(reaches(-offset)))
            def _():
                place[rows, :] = jnp.zeros((slots, lanes), f32)

    def exchange(turn, axis, send_from, land_in):
        is_wide = axis == "wide"
        count = wide_count if is_wide else narrow_count
        me = w if is_wide else n
        sends, recvs = (wide_send, wide_recv) if is_wide else (narrow_send, narrow_recv)

        def describe(peer, slot):
            return pltpu.make_async_remote_copy(
                src_ref=send_from(peer),
                dst_ref=land_in.at[slot],
                send_sem=sends.at[turn, peer],
                recv_sem=recvs.at[turn, slot],
                device_id=(peer, n) if is_wide else (w, peer),
                device_id_type=MESH,
            )

        def start():
            @pl.loop(1, count)
            def _(step):
                describe(lax.rem(me + step, count), me).start()

        def take():
            @pl.loop(1, count)
            def _(step):
                peer = lax.rem(me + step, count)
                describe(peer, peer).wait_recv()

        def finish():
            @pl.loop(1, count)
            def _(step):
                describe(lax.rem(me + step, count), me).wait_send()

        return start, take, finish

    residual_wide = exchange(0, "wide", lambda peer: partial.at[peer], wide_in)
    residual_narrow = exchange(0, "narrow", lambda peer: wide_sum, narrow_in)
    values_narrow = exchange(1, "narrow", lambda peer: value_mine, value_in)
    values_wide = exchange(1, "wide", lambda peer: coarse_mine, coarse_in)
    tops_narrow = exchange(2, "narrow", lambda peer: top_mine, top_narrow)
    tops_wide = exchange(2, "wide", lambda peer: top_half, top_wide)

    loads[0].wait()
    own[...] = rounded(pressure[...])
    pack(0, own)
    loads[1].wait()
    pack(1, conc)
    pl.semaphore_wait(barrier, wide_count + narrow_count - 2)
    send_margin(0)
    send_margin(1)

    @pl.loop(0, onehot.shape[1] // lanes)
    def _(chunk):
        numbers = lax.broadcasted_iota(jnp.int32, (onehot.shape[0], lanes), 1) + chunk * lanes
        hit = jnp.where(index_column[...] == numbers, 1.0, 0.0)
        onehot[:, pl.ds(pl.multiple_of(chunk * lanes, lanes), lanes)] = hit.astype(bf16)

    loads[2].wait()
    loads[3].wait()
    eye = lax.broadcasted_iota(jnp.int32, (lanes, lanes), 0) == lax.broadcasted_iota(jnp.int32, (lanes, lanes), 1)

    @pl.loop(0, extent)
    def _(row):
        block = matrix[row, 0].astype(f32)
        diag[pl.ds(row, 1), :] = jnp.sum(jnp.where(eye, block, 0.0), axis=0, keepdims=True)

    sub_id = lax.broadcasted_iota(jnp.int32, (8, lanes), 0)

    def product(group, vector):
        base = pl.multiple_of(group * 8, 8)
        for i in range(8):
            for k in range(4):
                picked[k, pl.ds(base + i, 1), :] = vector[pl.ds(sub_columns[base + i, k], 1), :]
        left = jnp.concatenate([picked[k, pl.ds(base, 8), :].astype(bf16) for k in range(4)], axis=1)
        total = jnp.zeros((8, lanes), f32)
        for i in range(8):
            blocks = jnp.concatenate([matrix[base + i, k] for k in range(4)], axis=1)
            made = lax.dot_general(left, blocks, contract_last, preferred_element_type=f32)
            total = jnp.where(sub_id == i, made, total)
        return total

    def groups_of(count, body):
        @pl.loop(0, count // 8)
        def _(group):
            body(group, pl.ds(pl.multiple_of(group * 8, 8), 8))

    ext_a[pl.ds(0, owned), :] = own[...]
    take_margin(0, ext_a)
    loads[4].wait()

    def residual_group(group, rows):
        own[rows, :] = rounded(right_side[rows, :] - product(group, ext_a))

    groups_of(owned, residual_group)
    pack(2, own)
    send_margin(2)

    loads[5].wait()
    flat = jnp.concatenate([own[pl.ds(b, 1), :] for b in range(owned)], axis=1)
    flat = jnp.broadcast_to(flat, (8, flat.shape[1])).astype(bf16)
    local_coarse = lax.dot_general(flat, basis[...], contract_last, preferred_element_type=f32)[0:1, :]
    high = rounded(local_coarse)
    middle = rounded(local_coarse - high)
    low = local_coarse - high - middle
    parts = jnp.concatenate([high, middle, low, jnp.zeros((5, low.shape[1]), f32)], axis=0).astype(bf16)

    @pl.loop(0, wide_count)
    def _(block):
        columns = pl.ds(pl.multiple_of(block * coarse_width, coarse_width), coarse_width)
        spread = lax.dot_general(parts, onehot[:, columns], plain, preferred_element_type=f32)
        partial[block] = jnp.sum(spread, axis=0, keepdims=True)

    residual_wide[0]()

    target[pl.ds(0, owned), :] = own[...]
    take_margin(2, target)
    ext_a[...] = target[...] / diag[...]

    def sweep(count, old, new):
        def body(group, rows):
            new[rows, :] = old[rows, :] + (target[rows, :] - product(group, old)) / diag[rows, :]

        groups_of(count, body)

    def total_of(count, me, mine, landed):
        def add(step, total):
            return total + landed[lax.rem(me + step, count)]

        return lax.fori_loop(1, count, add, mine)

    old, new = ext_a, ext_b
    for turn in range(1, SWEEPS):
        sweep(extent if turn < SWEEPS - 1 else owned, old, new)
        old, new = new, old
        if turn == 1:
            residual_wide[1]()
            wide_sum[...] = total_of(wide_count, w, partial[w], wide_in)
            residual_narrow[0]()
        if turn == 2:
            loads[6].wait()
            residual_narrow[1]()
            block_sum = total_of(narrow_count, n, wide_sum[...], narrow_in)
            block_sum = jnp.broadcast_to(block_sum, (8, coarse_width))
            values = lax.dot_general(
                block_sum, inverse[...], contract_last, precision=lax.Precision.HIGHEST, preferred_element_type=f32
            )[0:1, :]
            value_mine[...] = rounded(values)
            value_in[n] = value_mine[...]
            values_narrow[0]()
    update = old

    values_narrow[1]()
    coarse_mine[...] = jnp.concatenate([value_in[i] for i in range(narrow_count)], axis=1)
    coarse_in[w] = coarse_mine[...]
    values_wide[0]()

    ext_c[pl.ds(0, owned), :] = conc[...]
    take_margin(1, ext_c)

    def gather_faces(place, field):
        @pl.loop(0, owned)
        def _(b):
            for f in range(faces):
                place[b, pl.ds(f, 1), :] = field[pl.ds(face_neighbor[f, b], 1), :]

    gather_faces(near_c, ext_c)
    for load in loads[7:]:
        load.wait()

    values_wide[1]()
    coarse = jnp.concatenate([coarse_in[i] for i in range(wide_count)], axis=1)
    coarse = jnp.broadcast_to(coarse, (8, coarse.shape[1])).astype(bf16)
    chosen = lax.dot_general(coarse, onehot[...], contract_last, preferred_element_type=f32).astype(bf16)
    correction = lax.dot_general(chosen, basis[...], plain, preferred_element_type=f32)
    for b in range(owned):
        own[pl.ds(b, 1), :] = correction[0:1, b * lanes : (b + 1) * lanes]
    own[...] = pressure[...] + update[pl.ds(0, owned), :] + own[...]
    pack(3, own)
    send_margin(3)
    pressure_out[...] = own[...]
    target[pl.ds(0, owned), :] = own[...]
    take_margin(3, target)
    gather_faces(near_p, target)

    @pl.loop(0, owned)
    def _(b):
        row = pl.ds(b, 1)
        flux = trans[:, pl.ds(pl.multiple_of(b * lanes, lanes), lanes)] * (own[row, :] - near_p[b])
        outward, inward = jnp.maximum(flux, 0.0), jnp.minimum(flux, 0.0)
        adv[row, :] = jnp.sum(outward * conc[row, :] + inward * near_c[b], axis=0, keepdims=True)
        ext_b[row, :] = jnp.sum(outward, axis=0, keepdims=True)

    cell_rate = (ext_b[pl.ds(0, owned), :] + rate[...]) / volume[...]
    top_mine[...] = jnp.max(cell_rate, axis=0, keepdims=True)
    tops_narrow[0]()
    scaled = (rate[...] * (inject[...] - conc[...]) - adv[...]) / volume[...]

    def top_of(count, me, mine, landed):
        def larger(step, top):
            return jnp.maximum(top, landed[lax.rem(me + step, count)])

        return lax.fori_loop(1, count, larger, mine)

    tops_narrow[1]()
    top_half[...] = top_of(narrow_count, n, top_mine[...], top_narrow)
    tops_wide[0]()
    tops_wide[1]()
    top = top_of(wide_count, w, top_half[...], top_wide)
    time_step = courant / jnp.max(top, axis=1, keepdims=True)
    conc_out[...] = conc[...] + time_step * scaled

    for turn in range(4):
        for position, offset in enumerate(shift_offsets):
            @pl.when(reaches(offset))
            def _():
                margin_copy(turn, position).wait_send()
    for one in (residual_wide, residual_narrow, values_narrow, values_wide, tops_narrow, tops_wide):
        one[2]()


def solution(mesh):
    wide_count, narrow_count = mesh.shape["wide"], mesh.shape["narrow"]

    def local(
        pressure,
        right_side,
        concentration,
        pore_volume,
        well_rate,
        inject_conc,
        transmissibility,
        face_neighbor,
        sub_matrix,
        sub_columns,
        send_blocks,
        send_counts,
        basis_weights,
        coarse_index,
        coarse_inverse,
    ):
        owned, lanes = pressure.shape
        extent = sub_matrix.shape[0]
        slots = send_blocks.shape[-1]
        faces = face_neighbor.shape[0]
        functions = coarse_index.shape[0]
        coarse_rows, coarse_width = coarse_inverse.shape
        coarse_total = coarse_width * wide_count
        streamed = (
            pressure,
            right_side,
            concentration,
            pore_volume,
            well_rate,
            inject_conc,
            transmissibility,
            sub_matrix,
            basis_weights,
            coarse_inverse,
        )
        dma, vmem = pltpu.SemaphoreType.DMA, pltpu.VMEM
        field, ext = vmem((owned, lanes), f32), vmem((extent, lanes), f32)
        out = jax.ShapeDtypeStruct((owned, lanes), f32)
        return pl.pallas_call(
            functools.partial(kernel, wide_count, narrow_count),
            out_shape=(out, out),
            in_specs=[pl.BlockSpec(memory_space=pltpu.SMEM)] * 4
            + [pl.BlockSpec(memory_space=pltpu.VMEM)]
            + [pl.BlockSpec(memory_space=pl.ANY)] * len(streamed),
            out_specs=[pl.BlockSpec(memory_space=pltpu.VMEM)] * 2,
            scratch_shapes=[vmem(value.shape, value.dtype) for value in streamed]
            + [
                dma((11,)),
                vmem((4, 4, slots, lanes), f32),
                vmem((4, 4, slots, lanes), f32),
                dma((4, 4)),
                dma((4, 4)),
                field,
                ext,
                ext,
                ext,
                ext,
                vmem((4, extent, lanes), f32),
                vmem((functions, coarse_total), bf16),
                vmem((wide_count, 1, coarse_width), f32),
                vmem((wide_count, 1, coarse_width), f32),
                vmem((1, coarse_width), f32),
                vmem((narrow_count, 1, coarse_width), f32),
                vmem((narrow_count, 1, coarse_rows), f32),
                vmem((1, coarse_rows), f32),
                vmem((wide_count, 1, coarse_width), f32),
                vmem((1, coarse_width), f32),
                vmem((1, lanes), f32),
                vmem((narrow_count, 1, lanes), f32),
                vmem((1, lanes), f32),
                vmem((wide_count, 1, lanes), f32),
                dma((3, wide_count)),
                dma((3, wide_count)),
                dma((3, narrow_count)),
                dma((3, narrow_count)),
                vmem((owned, faces, lanes), f32),
                vmem((owned, faces, lanes), f32),
                ext,
                field,
            ],
            compiler_params=pltpu.CompilerParams(
                collective_id=0, has_side_effects=True, vmem_limit_bytes=48 << 20
            ),
            name="iteration",
        )(
            face_neighbor,
            sub_columns,
            send_blocks,
            send_counts,
            coarse_index.reshape(functions, 1),
            *streamed,
        )

    split = ("wide", "narrow")
    return jax.shard_map(
        local,
        mesh=mesh,
        in_specs=(
            P(split, None),
            P(split, None),
            P(split, None),
            P(split, None),
            P(split, None),
            P(split, None),
            P(None, split),
            P(None, split),
            P(split, None, None, None),
            P(split, None),
            P(split, None, None),
            P(split, None),
            P(split, None),
            P(split),
            P(split, None),
        ),
        out_specs=(P(split, None), P(split, None)),
        check_vma=False,
    )
```

time: 233 us -> 57.3 us (0.25)
  blocking collectives: 106 us -> 0 us
  Pallas kernels: 0 us -> 43.3 us
  starting transfers between devices: 42.3 us -> 0 us
  matrix products: 29.2 us -> 0 us
  between operations: 15.3 us -> 0.67 us
  waiting for transfers between devices: 10.2 us -> 0 us
  local copies, waits for them, and re-layouts: 21.3 us -> 12.6 us
  other arithmetic: 8.02 us -> 0 us
    pallas_call x0 -> x1, Pallas kernels: none -> 43.3 us  [local(): pl.pallas_call(functools.partial(kernel, wide_count, narrow_count), out_s...]
    ppermute x16 -> x0, starting transfers between devices: 42.3 us -> none  [from_behind(): lax.ppermute(value, axis, [(source, source + steps) for source in range(l...]
    psum x1 -> x0, blocking collectives: 40 us -> none  [local(): summed = lax.psum(partial_value, ('wide', 'narrow'))]
    pmax x1 -> x0, blocking collectives: 39.9 us -> none  [local(): rate_top = lax.pmax(jnp.max(cell_rate), ('wide', 'narrow'))]
    dot_general x8 -> x0, matrix products: 29.2 us -> none  [the longest x5 26 us: block_product(): jnp.einsum('rkij,rkj->ri', matrix, picked, preferred_element_type=jnp.flo...]
    all_gather x1 -> x0, blocking collectives: 26 us -> none  [local(): coarse_values = lax.all_gather(owner_values, 'wide', axis=0, tiled=True)]
    gather x15 -> x0, local copies, waits for them, and re-layouts: 11.8 us -> none  [the longest x5 4.13 us: block_product(): picked = vector_b[columns]]
    ppermute x16 -> x0, waiting for transfers between devices: 10.2 us -> none  [from_behind(): lax.ppermute(value, axis, [(source, source + steps) for source in range(l...]
  transfers between devices with their start and end apart: 17 -> 0, of which waited for: 4 -> 0; matrix products, arithmetic and copies ran while one was open for 21% -> 0% of each run, Pallas kernels for 0% -> 0%
where the time goes in v1:
time: 57.3 us; the launch traced here: 56.5 us
  Pallas kernels  43.3 us (76%)
  local copies, waits for them, and re-layouts  12.6 us (22%)
  between operations  0.67 us (1%)
    pallas_call x1, Pallas kernels, local(): pl.pallas_call(functools.partial(kernel, wide_count, narrow_count), out_s...  43.3 us
    unnamed x27, local copies, waits for them, and re-layouts  11.7 us

profile of v1, /device:TPU:0, one launch (start us, length us, event | category | flops | bytes accessed | tf_op | source)
XLA Modules:
  0.0 56.5 jit_solution(13149956479216779066)
XLA Ops:
  0.6 0.8 %copy.18.sub_columns = s32[64,4]{1,0:T(8,128)S(1)} copy(s32[64,4]{0,1:T(4,128)} %param.24) | data formatting | bytes 2048 | tf_op args[9]
  1.4 0.8 %copy.19.index_column = s32[256,1]{1,0:T(8,128)S(1)} copy(s32[256,1]{0,1:T(1,128)} %bitcast.1) | data formatting | bytes 2048 | tf_op jit(solution)/shard_map/reshape | solution.py:473
  2.2 0.0 copy-start
  2.2 1.6 %copy-done = bf16[256,4096]{1,0:T(8,128)(2,1)S(1)} copy-done((bf16[256,4096]{1,0:T(8,128)(2,1)S(1)}, bf16[256,4096]{1,0:T(8,128)(2,1)}, u32[]{:S(2)}) %copy-start) | copy-done | bytes 2097176
  3.8 0.0 copy-start.1
  3.8 0.9 %copy-done.1 = f32[128,512]{1,0:T(8,128)S(1)} copy-done((f32[128,512]{1,0:T(8,128)S(1)}, f32[128,512]{1,0:T(8,128)}, u32[]{:S(2)}) %copy-start.1) | copy-done | bytes 262168
  4.8 0.0 copy-start.2
  4.8 0.9 %copy-done.2 = f32[6,4096]{1,0:T(8,128)S(1)} copy-done((f32[6,4096]{1,0:T(8,128)S(1)}, f32[6,4096]{1,0:T(8,128)}, u32[]{:S(2)}) %copy-start.2) | copy-done | bytes 98328
  5.7 0.0 copy-start.3
  5.7 0.7 %copy-done.3 = f32[32,128]{1,0:T(8,128)S(1)} copy-done((f32[32,128]{1,0:T(8,128)S(1)}, f32[32,128]{1,0:T(8,128)}, u32[]{:S(2)}) %copy-start.3) | copy-done | bytes 16408
  6.4 0.0 copy-start.4
  6.4 0.7 %copy-done.4 = f32[32,128]{1,0:T(8,128)S(1)} copy-done((f32[32,128]{1,0:T(8,128)S(1)}, f32[32,128]{1,0:T(8,128)}, u32[]{:S(2)}) %copy-start.4) | copy-done | bytes 16408
  7.1 0.0 copy-start.5
  7.1 0.7 %copy-done.5 = f32[32,128]{1,0:T(8,128)S(1)} copy-done((f32[32,128]{1,0:T(8,128)S(1)}, f32[32,128]{1,0:T(8,128)}, u32[]{:S(2)}) %copy-start.5) | copy-done | bytes 16408
  7.8 0.0 copy-start.6
  7.8 0.7 %copy-done.6 = f32[32,128]{1,0:T(8,128)S(1)} copy-done((f32[32,128]{1,0:T(8,128)S(1)}, f32[32,128]{1,0:T(8,128)}, u32[]{:S(2)}) %copy-start.6) | copy-done | bytes 16408
  8.5 0.0 copy-start.7
  8.5 0.7 %copy-done.7 = f32[32,128]{1,0:T(8,128)S(1)} copy-done((f32[32,128]{1,0:T(8,128)S(1)}, f32[32,128]{1,0:T(8,128)}, u32[]{:S(2)}) %copy-start.7) | copy-done | bytes 16408
  9.3 0.0 copy-start.8
  9.3 0.7 %copy-done.8 = f32[32,128]{1,0:T(8,128)S(1)} copy-done((f32[32,128]{1,0:T(8,128)S(1)}, f32[32,128]{1,0:T(8,128)}, u32[]{:S(2)}) %copy-start.8) | copy-done | bytes 16408
  10.0 0.0 copy-start.9
  10.0 0.7 %copy-done.9 = s32[6,32]{1,0:T(8,128)S(1)} copy-done((s32[6,32]{1,0:T(8,128)S(1)}, s32[6,32]{1,0:T(8,128)}, u32[]{:S(2)}) %copy-start.9) | copy-done | bytes 792
  10.7 0.0 copy-start.10
  10.7 0.7 %copy-done.10 = s32[1,4,8]{2,1,0:T(4,128)S(1)} copy-done((s32[1,4,8]{2,1,0:T(4,128)S(1)}, s32[1,4,8]{2,1,0:T(4,128)}, u32[]{:S(2)}) %copy-start.10) | copy-done | bytes 152
  11.3 0.0 copy-start.11
  11.3 0.7 %copy-done.11 = s32[1,4]{1,0:T(1,128)S(1)} copy-done((s32[1,4]{1,0:T(1,128)S(1)}, s32[1,4]{1,0:T(1,128)}, u32[]{:S(2)}) %copy-start.11) | copy-done | bytes 40
  12.0 43.3 %iteration.1 = (f32[32,128]{1,0:T(8,128)S(1)}, f32[32,128]{1,0:T(8,128)S(1)}) custom-call(s32[6,32]{1,0:T(8,128)S(1)} %copy-done.9, s32[64,4]{1,0:T(8,128)S(1)} %copy.18.sub_columns, s32[1,4,8]{2,1,0:T(4,128)S(1)} %copy-done.10, s32[1,4]{1,0:T(1,128)S(1)} %copy-done.11, s32[256,1]{1,0:T(8,128)S(1)} %copy.19.index_column, f32[32,128]{1,0:T(8,128)S(1)} %copy-done.3, ...), custom_call_target="tpu_custom_call" | custom-call | tf_op jit(solution)/shard_map/iteration/pallas_call | solution.py:422
  55.3 0.6 %copy.22 = f32[32,128]{1,0:T(8,128)} copy(f32[32,128]{1,0:T(8,128)S(1)} %get-tuple-element.4) | data formatting | bytes 32768
  55.9 0.6 %copy.23 = f32[32,128]{1,0:T(8,128)} copy(f32[32,128]{1,0:T(8,128)S(1)} %get-tuple-element.5) | data formatting | bytes 32768
Async XLA Ops:
  2.2 1.6 %copy-start = (bf16[256,4096]{1,0:T(8,128)(2,1)S(1)}, bf16[256,4096]{1,0:T(8,128)(2,1)}, u32[]{:S(2)}) copy-start(bf16[256,4096]{1,0:T(8,128)(2,1)} %basis_hbm.1) | copy-start | bytes 6291460
  3.8 0.9 %copy-start.1 = (f32[128,512]{1,0:T(8,128)S(1)}, f32[128,512]{1,0:T(8,128)}, u32[]{:S(2)}) copy-start(f32[128,512]{1,0:T(8,128)} %inverse_hbm.1) | copy-start | bytes 786436
  4.8 0.9 %copy-start.2 = (f32[6,4096]{1,0:T(8,128)S(1)}, f32[6,4096]{1,0:T(8,128)}, u32[]{:S(2)}) copy-start(f32[6,4096]{1,0:T(8,128)} %trans_hbm.1) | copy-start | bytes 294916
  5.7 0.7 %copy-start.3 = (f32[32,128]{1,0:T(8,128)S(1)}, f32[32,128]{1,0:T(8,128)}, u32[]{:S(2)}) copy-start(f32[32,128]{1,0:T(8,128)} %pressure_hbm.1) | copy-start | bytes 49156
  6.4 0.7 %copy-start.4 = (f32[32,128]{1,0:T(8,128)S(1)}, f32[32,128]{1,0:T(8,128)}, u32[]{:S(2)}) copy-start(f32[32,128]{1,0:T(8,128)} %right_hbm.1) | copy-start | bytes 49156
  7.1 0.7 %copy-start.5 = (f32[32,128]{1,0:T(8,128)S(1)}, f32[32,128]{1,0:T(8,128)}, u32[]{:S(2)}) copy-start(f32[32,128]{1,0:T(8,128)} %conc_hbm.1) | copy-start | bytes 49156
  7.8 0.7 %copy-start.6 = (f32[32,128]{1,0:T(8,128)S(1)}, f32[32,128]{1,0:T(8,128)}, u32[]{:S(2)}) copy-start(f32[32,128]{1,0:T(8,128)} %volume_hbm.1) | copy-start | bytes 49156
  8.5 0.7 %copy-start.7 = (f32[32,128]{1,0:T(8,128)S(1)}, f32[32,128]{1,0:T(8,128)}, u32[]{:S(2)}) copy-start(f32[32,128]{1,0:T(8,128)} %rate_hbm.1) | copy-start | bytes 49156
  9.3 0.7 %copy-start.8 = (f32[32,128]{1,0:T(8,128)S(1)}, f32[32,128]{1,0:T(8,128)}, u32[]{:S(2)}) copy-start(f32[32,128]{1,0:T(8,128)} %inject_hbm.1) | copy-start | bytes 49156
  10.0 0.7 %copy-start.9 = (s32[6,32]{1,0:T(8,128)S(1)}, s32[6,32]{1,0:T(8,128)}, u32[]{:S(2)}) copy-start(s32[6,32]{1,0:T(8,128)} %face_neighbor.1) | copy-start | bytes 2308
  10.7 0.7 %copy-start.10 = (s32[1,4,8]{2,1,0:T(4,128)S(1)}, s32[1,4,8]{2,1,0:T(4,128)}, u32[]{:S(2)}) copy-start(s32[1,4,8]{2,1,0:T(4,128)} %send_blocks.1) | copy-start | bytes 388
  11.3 0.7 %copy-start.11 = (s32[1,4]{1,0:T(1,128)S(1)}, s32[1,4]{1,0:T(1,128)}, u32[]{:S(2)}) copy-start(s32[1,4]{1,0:T(1,128)} %send_counts.1) | copy-start | bytes 52

commit v2 on v1

--- a/solution.py
+++ b/solution.py
@@ -28,7 +28,7 @@
     sub_columns,
     send_blocks,
     send_counts,
-    index_column,
+    index_row,
     pressure_hbm,
     right_hbm,
     conc_hbm,
@@ -64,27 +64,20 @@
     picked,
     onehot,
     partial,
-    wide_in,
-    wide_sum,
-    narrow_in,
+    residual_in,
     value_in,
     value_mine,
-    coarse_in,
-    coarse_mine,
     top_mine,
-    top_narrow,
-    top_half,
-    top_wide,
-    wide_send,
-    wide_recv,
-    narrow_send,
-    narrow_recv,
+    top_in,
+    all_send,
+    all_recv,
     near_p,
     near_c,
     ext_c,
     adv,
 ):
     w, n = lax.axis_index("wide"), lax.axis_index("narrow")
+    devices, me = wide_count * narrow_count, w * narrow_count + n
     owned, lanes = pressure.shape
     extent = ext_a.shape[0]
     slots = outbox.shape[2]
@@ -111,10 +104,12 @@
         loads.append(copy)
 
     barrier = pltpu.get_barrier_semaphore()
-    for step in range(1, wide_count):
-        pl.semaphore_signal(barrier, inc=1, device_id=(lax.rem(w + step, wide_count), n), device_id_type=MESH)
-    for step in range(1, narrow_count):
-        pl.semaphore_signal(barrier, inc=1, device_id=(w, lax.rem(n + step, narrow_count)), device_id_type=MESH)
+
+    @pl.loop(1, devices)
+    def _(step):
+        peer = lax.rem(me + step, devices)
+        pl.semaphore_signal(barrier, inc=1, device_id=(peer // narrow_count, lax.rem(peer, narrow_count)), device_id_type=MESH)
+
 
     def margin_copy(turn, position):
         offset = shift_offsets[position]
@@ -158,61 +153,53 @@
             def _():
                 place[rows, :] = jnp.zeros((slots, lanes), f32)
 
-    def exchange(turn, axis, send_from, land_in):
-        is_wide = axis == "wide"
-        count = wide_count if is_wide else narrow_count
-        me = w if is_wide else n
-        sends, recvs = (wide_send, wide_recv) if is_wide else (narrow_send, narrow_recv)
-
+    def exchange(turn, send_from, land_in):
         def describe(peer, slot):
             return pltpu.make_async_remote_copy(
                 src_ref=send_from(peer),
                 dst_ref=land_in.at[slot],
-                send_sem=sends.at[turn, peer],
-                recv_sem=recvs.at[turn, slot],
-                device_id=(peer, n) if is_wide else (w, peer),
+                send_sem=all_send.at[turn, peer],
+                recv_sem=all_recv.at[turn, slot],
+                device_id=(peer // narrow_count, lax.rem(peer, narrow_count)),
                 device_id_type=MESH,
             )
 
         def start():
-            @pl.loop(1, count)
+            @pl.loop(1, devices)
             def _(step):
-                describe(lax.rem(me + step, count), me).start()
+                describe(lax.rem(me + step, devices), me).start()
 
         def take():
-            @pl.loop(1, count)
+            @pl.loop(1, devices)
             def _(step):
-                peer = lax.rem(me + step, count)
+                peer = lax.rem(me + step, devices)
                 describe(peer, peer).wait_recv()
 
         def finish():
-            @pl.loop(1, count)
+            @pl.loop(1, devices)
             def _(step):
-                describe(lax.rem(me + step, count), me).wait_send()
+                describe(lax.rem(me + step, devices), me).wait_send()
 
         return start, take, finish
 
-    residual_wide = exchange(0, "wide", lambda peer: partial.at[peer], wide_in)
-    residual_narrow = exchange(0, "narrow", lambda peer: wide_sum, narrow_in)
-    values_narrow = exchange(1, "narrow", lambda peer: value_mine, value_in)
-    values_wide = exchange(1, "wide", lambda peer: coarse_mine, coarse_in)
-    tops_narrow = exchange(2, "narrow", lambda peer: top_mine, top_narrow)
-    tops_wide = exchange(2, "wide", lambda peer: top_half, top_wide)
+    residuals = exchange(0, lambda peer: partial.at[peer // narrow_count], residual_in)
+    values_all = exchange(1, lambda peer: value_mine, value_in)
+    tops = exchange(2, lambda peer: top_mine, top_in)
+
+    @pl.loop(0, onehot.shape[0] // lanes)
+    def _(chunk):
+        numbers = lax.broadcasted_iota(jnp.int32, (lanes, onehot.shape[1]), 0) + chunk * lanes
+        hit = jnp.where(index_row[...] == numbers, 1.0, 0.0)
+        onehot[pl.ds(pl.multiple_of(chunk * lanes, lanes), lanes), :] = hit.astype(bf16)
 
     loads[0].wait()
     own[...] = rounded(pressure[...])
     pack(0, own)
+    pl.semaphore_wait(barrier, devices - 1)
+    send_margin(0)
     loads[1].wait()
     pack(1, conc)
-    pl.semaphore_wait(barrier, wide_count + narrow_count - 2)
-    send_margin(0)
     send_margin(1)
-
-    @pl.loop(0, onehot.shape[1] // lanes)
-    def _(chunk):
-        numbers = lax.broadcasted_iota(jnp.int32, (onehot.shape[0], lanes), 1) + chunk * lanes
-        hit = jnp.where(index_column[...] == numbers, 1.0, 0.0)
-        onehot[:, pl.ds(pl.multiple_of(chunk * lanes, lanes), lanes)] = hit.astype(bf16)
 
     loads[2].wait()
     loads[3].wait()
@@ -229,7 +216,7 @@
         base = pl.multiple_of(group * 8, 8)
         for i in range(8):
             for k in range(4):
-                picked[k, pl.ds(base + i, 1), :] = vector[pl.ds(sub_columns[base + i, k], 1), :]
+                picked[k, pl.ds(base + i, 1), :] = vector[pl.ds(sub_columns[k, base + i], 1), :]
         left = jnp.concatenate([picked[k, pl.ds(base, 8), :].astype(bf16) for k in range(4)], axis=1)
         total = jnp.zeros((8, lanes), f32)
         for i in range(8):
@@ -266,10 +253,10 @@
     @pl.loop(0, wide_count)
     def _(block):
         columns = pl.ds(pl.multiple_of(block * coarse_width, coarse_width), coarse_width)
-        spread = lax.dot_general(parts, onehot[:, columns], plain, preferred_element_type=f32)
+        spread = lax.dot_general(parts, onehot[columns, :], contract_last, preferred_element_type=f32)
         partial[block] = jnp.sum(spread, axis=0, keepdims=True)
 
-    residual_wide[0]()
+    residuals[0]()
 
     target[pl.ds(0, owned), :] = own[...]
     take_margin(2, target)
@@ -280,38 +267,23 @@
             new[rows, :] = old[rows, :] + (target[rows, :] - product(group, old)) / diag[rows, :]
 
         groups_of(count, body)
-
-    def total_of(count, me, mine, landed):
-        def add(step, total):
-            return total + landed[lax.rem(me + step, count)]
-
-        return lax.fori_loop(1, count, add, mine)
 
     old, new = ext_a, ext_b
     for turn in range(1, SWEEPS):
         sweep(extent if turn < SWEEPS - 1 else owned, old, new)
         old, new = new, old
-        if turn == 1:
-            residual_wide[1]()
-            wide_sum[...] = total_of(wide_count, w, partial[w], wide_in)
-            residual_narrow[0]()
         if turn == 2:
             loads[6].wait()
-            residual_narrow[1]()
-            block_sum = total_of(narrow_count, n, wide_sum[...], narrow_in)
-            block_sum = jnp.broadcast_to(block_sum, (8, coarse_width))
+            residual_in[me] = partial[w]
+            residuals[1]()
+            block_sum = jnp.broadcast_to(jnp.sum(residual_in[...], axis=0), (8, coarse_width))
             values = lax.dot_general(
                 block_sum, inverse[...], contract_last, precision=lax.Precision.HIGHEST, preferred_element_type=f32
             )[0:1, :]
             value_mine[...] = rounded(values)
-            value_in[n] = value_mine[...]
-            values_narrow[0]()
+            value_in[me] = value_mine[...]
+            values_all[0]()
     update = old
-
-    values_narrow[1]()
-    coarse_mine[...] = jnp.concatenate([value_in[i] for i in range(narrow_count)], axis=1)
-    coarse_in[w] = coarse_mine[...]
-    values_wide[0]()
 
     ext_c[pl.ds(0, owned), :] = conc[...]
     take_margin(1, ext_c)
@@ -326,10 +298,10 @@
     for load in loads[7:]:
         load.wait()
 
-    values_wide[1]()
-    coarse = jnp.concatenate([coarse_in[i] for i in range(wide_count)], axis=1)
+    values_all[1]()
+    coarse = jnp.concatenate([value_in[i] for i in range(devices)], axis=1)
     coarse = jnp.broadcast_to(coarse, (8, coarse.shape[1])).astype(bf16)
-    chosen = lax.dot_general(coarse, onehot[...], contract_last, preferred_element_type=f32).astype(bf16)
+    chosen = lax.dot_general(coarse, onehot[...], plain, preferred_element_type=f32).astype(bf16)
     correction = lax.dot_general(chosen, basis[...], plain, preferred_element_type=f32)
     for b in range(owned):
         own[pl.ds(b, 1), :] = correction[0:1, b * lanes : (b + 1) * lanes]
@@ -351,20 +323,12 @@
 
     cell_rate = (ext_b[pl.ds(0, owned), :] + rate[...]) / volume[...]
     top_mine[...] = jnp.max(cell_rate, axis=0, keepdims=True)
-    tops_narrow[0]()
+    tops[0]()
     scaled = (rate[...] * (inject[...] - conc[...]) - adv[...]) / volume[...]
 
-    def top_of(count, me, mine, landed):
-        def larger(step, top):
-            return jnp.maximum(top, landed[lax.rem(me + step, count)])
-
-        return lax.fori_loop(1, count, larger, mine)
-
-    tops_narrow[1]()
-    top_half[...] = top_of(narrow_count, n, top_mine[...], top_narrow)
-    tops_wide[0]()
-    tops_wide[1]()
-    top = top_of(wide_count, w, top_half[...], top_wide)
+    top_in[me] = top_mine[...]
+    tops[1]()
+    top = jnp.max(top_in[...], axis=0)
     time_step = courant / jnp.max(top, axis=1, keepdims=True)
     conc_out[...] = conc[...] + time_step * scaled
 
@@ -373,7 +337,7 @@
             @pl.when(reaches(offset))
             def _():
                 margin_copy(turn, position).wait_send()
-    for one in (residual_wide, residual_narrow, values_narrow, values_wide, tops_narrow, tops_wide):
+    for one in (residuals, values_all, tops):
         one[2]()
 
 
@@ -404,6 +368,7 @@
         functions = coarse_index.shape[0]
         coarse_rows, coarse_width = coarse_inverse.shape
         coarse_total = coarse_width * wide_count
+        devices = wide_count * narrow_count
         streamed = (
             pressure,
             right_side,
@@ -424,7 +389,7 @@
             out_shape=(out, out),
             in_specs=[pl.BlockSpec(memory_space=pltpu.SMEM)] * 4
             + [pl.BlockSpec(memory_space=pltpu.VMEM)]
-            + [pl.BlockSpec(memory_space=pl.ANY)] * len(streamed),
+            + [pl.BlockSpec(memory_space=pltpu.HBM)] * len(streamed),
             out_specs=[pl.BlockSpec(memory_space=pltpu.VMEM)] * 2,
             scratch_shapes=[vmem(value.shape, value.dtype) for value in streamed]
             + [
@@ -439,38 +404,30 @@
                 ext,
                 ext,
                 vmem((4, extent, lanes), f32),
-                vmem((functions, coarse_total), bf16),
+                vmem((coarse_total, functions), bf16),
                 vmem((wide_count, 1, coarse_width), f32),
-                vmem((wide_count, 1, coarse_width), f32),
-                vmem((1, coarse_width), f32),
-                vmem((narrow_count, 1, coarse_width), f32),
-                vmem((narrow_count, 1, coarse_rows), f32),
+                vmem((devices, 1, coarse_width), f32),
+                vmem((devices, 1, coarse_rows), f32),
                 vmem((1, coarse_rows), f32),
-                vmem((wide_count, 1, coarse_width), f32),
-                vmem((1, coarse_width), f32),
                 vmem((1, lanes), f32),
-                vmem((narrow_count, 1, lanes), f32),
-                vmem((1, lanes), f32),
-                vmem((wide_count, 1, lanes), f32),
-                dma((3, wide_count)),
-                dma((3, wide_count)),
-                dma((3, narrow_count)),
-                dma((3, narrow_count)),
+                vmem((devices, 1, lanes), f32),
+                dma((3, devices)),
+                dma((3, devices)),
                 vmem((owned, faces, lanes), f32),
                 vmem((owned, faces, lanes), f32),
                 ext,
                 field,
             ],
             compiler_params=pltpu.CompilerParams(
-                collective_id=0, has_side_effects=True, vmem_limit_bytes=48 << 20
+                collective_id=0, has_side_effects=True, vmem_limit_bytes=60 << 20
             ),
             name="iteration",
         )(
             face_neighbor,
-            sub_columns,
+            sub_columns.T,
             send_blocks,
             send_counts,
-            coarse_index.reshape(functions, 1),
+            coarse_index.reshape(1, functions),
             *streamed,
         )
 

time: 57.3 us -> 44.3 us (0.77)
  local copies, waits for them, and re-layouts: 12.6 us -> 2.65 us
  Pallas kernels: 43.3 us -> 40.7 us
    unnamed x27 -> x2, local copies, waits for them, and re-layouts: 11.7 us -> 2.65 us
    pallas_call x1, Pallas kernels: 43.3 us -> 40.7 us  [local(): pl.pallas_call(functools.partial(kernel, wide_count, narrow_count), out_s...]
    reshape x1 -> x0, local copies, waits for them, and re-layouts: 0.8 us -> none  [local(): coarse_index.reshape(functions, 1)]
where the time goes in v2:
time: 44.3 us; the launch traced here: 44 us
  Pallas kernels  40.7 us (92%)
  local copies, waits for them, and re-layouts  2.65 us (6%)
  between operations  0.64 us (1%)
    pallas_call x1, Pallas kernels, local(): pl.pallas_call(functools.partial(kernel, wide_count, narrow_count), out_s...  40.7 us
    unnamed x2, local copies, waits for them, and re-layouts  2.65 us

profile of v2, /device:TPU:0, one launch (start us, length us, event | category | flops | bytes accessed | tf_op | source)
XLA Modules:
  0.0 44.0 jit_solution(7636322049410872669)
XLA Ops:
  0.6 40.7 %iteration.1 = (f32[32,128]{1,0:T(8,128)}, f32[32,128]{1,0:T(8,128)}) custom-call(s32[6,32]{1,0:T(8,128)} %face_neighbor.1, s32[4,64]{1,0:T(4,128)} %bitcast.2, s32[1,4,8]{2,1,0:T(4,128)} %send_blocks.1, s32[1,4]{1,0:T(1,128)} %send_counts.1, s32[1,256]{1,0:T(1,128)} %bitcast.3, f32[32,128]{1,0:T(8,128)} %pressure_hbm.1, f32[32,128]{1,0:T(8,128)} %right_hbm.1, ...), custom_call_target="tpu_custom_call" | custom-call | tf_op jit(solution)/shard_map/iteration/pallas_call | solution.py:387
  41.3 1.3 %copy.19 = f32[32,128]{1,0:T(8,128)} copy(f32[32,128]{1,0:T(8,128)} %get-tuple-element.4) | data formatting | bytes 32768
  42.6 1.3 %copy.20 = f32[32,128]{1,0:T(8,128)} copy(f32[32,128]{1,0:T(8,128)} %get-tuple-element.5) | data formatting | bytes 32768

commit v3 on v2

--- a/solution.py
+++ b/solution.py
@@ -105,11 +105,21 @@
 
     barrier = pltpu.get_barrier_semaphore()
 
-    @pl.loop(1, devices)
-    def _(step):
-        peer = lax.rem(me + step, devices)
-        pl.semaphore_signal(barrier, inc=1, device_id=(peer // narrow_count, lax.rem(peer, narrow_count)), device_id_type=MESH)
-
+    def wrapped(at, count):
+        return jnp.where(at >= count, at - count, at)
+
+    def each_other(body):
+        columns = [n] + [wrapped(n + step, narrow_count) for step in range(1, narrow_count)]
+        for column in columns[1:]:
+            body(w, column)
+
+        @pl.loop(1, wide_count)
+        def _(step):
+            row = wrapped(w + step, wide_count)
+            for column in columns:
+                body(row, column)
+
+    each_other(lambda row, column: pl.semaphore_signal(barrier, inc=1, device_id=(row, column), device_id_type=MESH))
 
     def margin_copy(turn, position):
         offset = shift_offsets[position]
@@ -154,37 +164,33 @@
                 place[rows, :] = jnp.zeros((slots, lanes), f32)
 
     def exchange(turn, send_from, land_in):
-        def describe(peer, slot):
-            return pltpu.make_async_remote_copy(
-                src_ref=send_from(peer),
-                dst_ref=land_in.at[slot],
-                send_sem=all_send.at[turn, peer],
-                recv_sem=all_recv.at[turn, slot],
-                device_id=(peer // narrow_count, lax.rem(peer, narrow_count)),
-                device_id_type=MESH,
-            )
-
         def start():
-            @pl.loop(1, devices)
-            def _(step):
-                describe(lax.rem(me + step, devices), me).start()
-
-        def take():
-            @pl.loop(1, devices)
-            def _(step):
-                peer = lax.rem(me + step, devices)
-                describe(peer, peer).wait_recv()
-
-        def finish():
-            @pl.loop(1, devices)
-            def _(step):
-                describe(lax.rem(me + step, devices), me).wait_send()
-
-        return start, take, finish
-
-    residuals = exchange(0, lambda peer: partial.at[peer // narrow_count], residual_in)
-    values_all = exchange(1, lambda peer: value_mine, value_in)
-    tops = exchange(2, lambda peer: top_mine, top_in)
+            def send(row, column):
+                pltpu.make_async_remote_copy(
+                    src_ref=send_from(row),
+                    dst_ref=land_in.at[me],
+                    send_sem=all_send.at[turn],
+                    recv_sem=all_recv.at[turn],
+                    device_id=(row, column),
+                    device_id_type=MESH,
+                ).start()
+
+            each_other(send)
+
+        others = land_in.at[pl.ds(0, devices - 1)]
+        every = pltpu.make_async_remote_copy(
+            src_ref=others,
+            dst_ref=others,
+            send_sem=all_send.at[turn],
+            recv_sem=all_recv.at[turn],
+            device_id=(wrapped(w + 1, wide_count), n),
+            device_id_type=MESH,
+        )
+        return start, every.wait_recv, every.wait_send
+
+    residuals = exchange(0, lambda row: partial.at[row], residual_in)
+    values_all = exchange(1, lambda row: value_mine, value_in)
+    tops = exchange(2, lambda row: top_mine, top_in)
 
     @pl.loop(0, onehot.shape[0] // lanes)
     def _(chunk):
@@ -219,10 +225,12 @@
                 picked[k, pl.ds(base + i, 1), :] = vector[pl.ds(sub_columns[k, base + i], 1), :]
         left = jnp.concatenate([picked[k, pl.ds(base, 8), :].astype(bf16) for k in range(4)], axis=1)
         total = jnp.zeros((8, lanes), f32)
-        for i in range(8):
-            blocks = jnp.concatenate([matrix[base + i, k] for k in range(4)], axis=1)
+        for i in range(0, 8, 2):
+            pair = matrix[pl.ds(base + i, 2)]
+            blocks = jnp.concatenate([pair[:, k].reshape(2 * lanes, lanes) for k in range(4)], axis=1)
             made = lax.dot_general(left, blocks, contract_last, preferred_element_type=f32)
-            total = jnp.where(sub_id == i, made, total)
+            total = jnp.where(sub_id == i, made[:, :lanes], total)
+            total = jnp.where(sub_id == i + 1, made[:, lanes:], total)
         return total
 
     def groups_of(count, body):
@@ -411,8 +419,8 @@
                 vmem((1, coarse_rows), f32),
                 vmem((1, lanes), f32),
                 vmem((devices, 1, lanes), f32),
-                dma((3, devices)),
-                dma((3, devices)),
+                dma((3,)),
+                dma((3,)),
                 vmem((owned, faces, lanes), f32),
                 vmem((owned, faces, lanes), f32),
                 ext,

time: 44.3 us -> 40.6 us (0.916)
  Pallas kernels: 40.7 us -> 36.9 us
    pallas_call x1, Pallas kernels: 40.7 us -> 36.9 us  [local(): pl.pallas_call(functools.partial(kernel, wide_count, narrow_count), out_s...]
where the time goes in v3:
time: 40.6 us; the launch traced here: 40.2 us
  Pallas kernels  36.9 us (91%)
  local copies, waits for them, and re-layouts  2.65 us (7%)
  between operations  0.64 us (2%)
    pallas_call x1, Pallas kernels, local(): pl.pallas_call(functools.partial(kernel, wide_count, narrow_count), out_s...  36.9 us
    unnamed x2, local copies, waits for them, and re-layouts  2.65 us

profile of v3, /device:TPU:0, one launch (start us, length us, event | category | flops | bytes accessed | tf_op | source)
XLA Modules:
  0.0 40.2 jit_solution(3315111815163940461)
XLA Ops:
  0.6 36.9 %iteration.1 = (f32[32,128]{1,0:T(8,128)}, f32[32,128]{1,0:T(8,128)}) custom-call(s32[6,32]{1,0:T(8,128)} %face_neighbor.1, s32[4,64]{1,0:T(4,128)} %bitcast.2, s32[1,4,8]{2,1,0:T(4,128)} %send_blocks.1, s32[1,4]{1,0:T(1,128)} %send_counts.1, s32[1,256]{1,0:T(1,128)} %bitcast.3, f32[32,128]{1,0:T(8,128)} %pressure_hbm.1, f32[32,128]{1,0:T(8,128)} %right_hbm.1, ...), custom_call_target="tpu_custom_call" | custom-call | tf_op jit(solution)/shard_map/iteration/pallas_call | solution.py:395
  37.5 1.3 %copy.19 = f32[32,128]{1,0:T(8,128)} copy(f32[32,128]{1,0:T(8,128)} %get-tuple-element.4) | data formatting | bytes 32768
  38.9 1.3 %copy.20 = f32[32,128]{1,0:T(8,128)} copy(f32[32,128]{1,0:T(8,128)} %get-tuple-element.5) | data formatting | bytes 32768

commit v4 on v3

--- a/solution.py
+++ b/solution.py
@@ -192,7 +192,7 @@
     values_all = exchange(1, lambda row: value_mine, value_in)
     tops = exchange(2, lambda row: top_mine, top_in)
 
-    @pl.loop(0, onehot.shape[0] // lanes)
+    @pl.loop(0, onehot.shape[0] // lanes, unroll=2)
     def _(chunk):
         numbers = lax.broadcasted_iota(jnp.int32, (lanes, onehot.shape[1]), 0) + chunk * lanes
         hit = jnp.where(index_row[...] == numbers, 1.0, 0.0)
@@ -211,7 +211,7 @@
     loads[3].wait()
     eye = lax.broadcasted_iota(jnp.int32, (lanes, lanes), 0) == lax.broadcasted_iota(jnp.int32, (lanes, lanes), 1)
 
-    @pl.loop(0, extent)
+    @pl.loop(0, extent, unroll=4)
     def _(row):
         block = matrix[row, 0].astype(f32)
         diag[pl.ds(row, 1), :] = jnp.sum(jnp.where(eye, block, 0.0), axis=0, keepdims=True)
@@ -234,7 +234,7 @@
         return total
 
     def groups_of(count, body):
-        @pl.loop(0, count // 8)
+        @pl.loop(0, count // 8, unroll=2)
         def _(group):
             body(group, pl.ds(pl.multiple_of(group * 8, 8), 8))
 
@@ -258,7 +258,7 @@
     low = local_coarse - high - middle
     parts = jnp.concatenate([high, middle, low, jnp.zeros((5, low.shape[1]), f32)], axis=0).astype(bf16)
 
-    @pl.loop(0, wide_count)
+    @pl.loop(0, wide_count, unroll=4)
     def _(block):
         columns = pl.ds(pl.multiple_of(block * coarse_width, coarse_width), coarse_width)
         spread = lax.dot_general(parts, onehot[columns, :], contract_last, preferred_element_type=f32)
@@ -297,7 +297,7 @@
     take_margin(1, ext_c)
 
     def gather_faces(place, field):
-        @pl.loop(0, owned)
+        @pl.loop(0, owned, unroll=4)
         def _(b):
             for f in range(faces):
                 place[b, pl.ds(f, 1), :] = field[pl.ds(face_neighbor[f, b], 1), :]
@@ -321,7 +321,7 @@
     take_margin(3, target)
     gather_faces(near_p, target)
 
-    @pl.loop(0, owned)
+    @pl.loop(0, owned, unroll=4)
     def _(b):
         row = pl.ds(b, 1)
         flux = trans[:, pl.ds(pl.multiple_of(b * lanes, lanes), lanes)] * (own[row, :] - near_p[b])

time: 40.6 us -> 38.9 us (0.958)
  Pallas kernels: 36.9 us -> 35.2 us
    pallas_call x1, Pallas kernels: 36.9 us -> 35.2 us  [local(): pl.pallas_call(functools.partial(kernel, wide_count, narrow_count), out_s...]
where the time goes in v4:
time: 38.9 us; the launch traced here: 38.5 us
  Pallas kernels  35.2 us (90%)
  local copies, waits for them, and re-layouts  2.65 us (7%)
  between operations  0.64 us (2%)
    pallas_call x1, Pallas kernels, local(): pl.pallas_call(functools.partial(kernel, wide_count, narrow_count), out_s...  35.2 us
    unnamed x2, local copies, waits for them, and re-layouts  2.65 us

profile of v4, /device:TPU:0, one launch (start us, length us, event | category | flops | bytes accessed | tf_op | source)
XLA Modules:
  0.0 38.5 jit_solution(10518651674378137090)
XLA Ops:
  0.6 35.2 %iteration.1 = (f32[32,128]{1,0:T(8,128)}, f32[32,128]{1,0:T(8,128)}) custom-call(s32[6,32]{1,0:T(8,128)} %face_neighbor.1, s32[4,64]{1,0:T(4,128)} %bitcast.2, s32[1,4,8]{2,1,0:T(4,128)} %send_blocks.1, s32[1,4]{1,0:T(1,128)} %send_counts.1, s32[1,256]{1,0:T(1,128)} %bitcast.3, f32[32,128]{1,0:T(8,128)} %pressure_hbm.1, f32[32,128]{1,0:T(8,128)} %right_hbm.1, ...), custom_call_target="tpu_custom_call" | custom-call | tf_op jit(solution)/shard_map/iteration/pallas_call | solution.py:395
  35.9 1.3 %copy.19 = f32[32,128]{1,0:T(8,128)} copy(f32[32,128]{1,0:T(8,128)} %get-tuple-element.4) | data formatting | bytes 32768
  37.2 1.3 %copy.20 = f32[32,128]{1,0:T(8,128)} copy(f32[32,128]{1,0:T(8,128)} %get-tuple-element.5) | data formatting | bytes 32768
